TPU v7x, 512 devices: a whole 4x4x16 slice. The times are simulated.
512 devices in a mesh: row: 16 (over y_lo, x, core), col: 32 (over z, y_hi).
Axes of the slice: x: 4, y: 4 (y_hi: 2, y_lo: 2; y = y_hi * 2 + y_lo), z: 16, core: 2. Of those that a mesh axis runs over, the one named last changes fastest.
Arguments:
- coefficients: float32 [8, 8192, 8192], P(None, 'row', 'col'), may hold values from -40 to 40, as said below
- lambdas: float32 [256], replicated, may hold values from -0.95 to 0.95
- right_vecs: float32 [8192, 256], P(('col', 'row')), may hold values from -6 to 6
- left_vecs: float32 [8192, 256], P(('row', 'col')), may hold values from -6 to 6
Outputs:
- right_resid: float32 [8192, 256], P(('row', 'col'))
- left_resid: float32 [8192, 256], P(('col', 'row'))
- root_mean: float32 [2, 256], replicated
Inputs may be any that keep to these rules, and one draw needn't show every extreme that they name: `coefficients`: the entries of every coefficient matrix.
All inputs are finite; a program needn't handle non-finite values.
Results may differ from a plain program's by a relative error of at most 0.0001.
Values sent between devices are 32-bit elements; how exact they have to be, the bound alone decides.
A program may use at most 64 MiB of HBM per device.

v0:
```python
import jax
import jax.numpy as jnp
from jax import lax
from jax.sharding import PartitionSpec as P

N = 8192
epsilon = 1e-06


def chebyshev(lambdas, count):
    terms = [jnp.ones_like(lambdas), lambdas]
    while len(terms) < count:
        terms.append(2.0 * lambdas * terms[-1] - terms[-2])
    return jnp.stack(terms[:count])


def right_term(matrices, weighted):
    total = jnp.dot(
        matrices[0],
        weighted[0],
        precision=lax.Precision.HIGHEST,
        preferred_element_type=jnp.float32,
    )
    for term in range(1, matrices.shape[0]):
        total = total + jnp.dot(
            matrices[term],
            weighted[term],
            precision=lax.Precision.HIGHEST,
            preferred_element_type=jnp.float32,
        )
    return total


def left_term(matrices, weighted):
    numbers = (((0,), (0,)), ((), ()))
    total = lax.dot_general(
        matrices[0],
        weighted[0],
        numbers,
        precision=lax.Precision.HIGHEST,
        preferred_element_type=jnp.float32,
    )
    for term in range(1, matrices.shape[0]):
        total = total + lax.dot_general(
            matrices[term],
            weighted[term],
            numbers,
            precision=lax.Precision.HIGHEST,
            preferred_element_type=jnp.float32,
        )
    return total


def body(coefficients, lambdas, right_vecs, left_vecs):
    weights = chebyshev(lambdas, coefficients.shape[0])
    right_cols = lax.all_gather(right_vecs, "row", axis=0, tiled=True)
    left_rows = lax.all_gather(left_vecs, "col", axis=0, tiled=True)
    right_weighted = right_cols[None, :, :] * weights[:, None, :]
    left_weighted = left_rows[None, :, :] * weights[:, None, :]
    matrices = coefficients
    right_resid = lax.psum_scatter(
        right_term(matrices, right_weighted), "col", scatter_dimension=0, tiled=True
    )
    matrices = coefficients
    left_resid = lax.psum_scatter(
        left_term(matrices, left_weighted), "row", scatter_dimension=0, tiled=True
    )
    right_squares, left_squares = lax.psum(
        (jnp.sum(right_resid * right_resid, axis=0), jnp.sum(left_resid * left_resid, axis=0)),
        ("row", "col"),
    )
    root_mean = jnp.sqrt(jnp.stack([right_squares, left_squares]) / N + epsilon)
    return (right_resid, left_resid, root_mean)


def solution(mesh):
    return jax.shard_map(
        body,
        mesh=mesh,
        in_specs=(P(None, "row", "col"), P(), P(("col", "row"), None), P(("row", "col"), None)),
        out_specs=(P(("row", "col"), None), P(("col", "row"), None), P()),
        check_vma=False,
    )
```

profile of v0, /device:TPU:1, one launch (start us, length us, event | category | flops | bytes accessed | tf_op | source)
XLA Modules:
  0.0 924.4 jit_solution(9988181470796313399)
XLA Ops:
  7.2 0.0 reduce-scatter.9.cloned.1.call-start
  7.2 0.7 multiply_subtract_fusion
  7.9 0.7 multiply_subtract_fusion.1
  8.6 72.7 %all_gather.7 = f32[512,256]{1,0:T(8,128)S(1)} all-gather(f32[16,256]{1,0:T(8,128)} %param.7), channel_id=1, replica_groups=mesh['row'=16,'col'=32] {'col'}, dimensions={0}, use_global_device_ids=true | all-gather | bytes 540672 | tf_op jit(solution)/shard_map/all_gather | solution.py:57
  81.3 0.7 stack.40
  82.0 0.0 copy-start
  82.0 0.4 broadcast_multiply_fusion
  82.4 1.8 copy-done
  84.2 1.0 fusion.2
  85.3 1.0 convolution_add_fusion.13
  86.3 1.0 convolution_add_fusion.12
  87.3 0.0 copy-start.2
  87.3 1.0 convolution_add_fusion.11
  88.4 1.0 convolution_add_fusion.10
  89.4 1.0 convolution_add_fusion.9
  90.4 1.0 convolution_add_fusion.8
  91.5 1.0 fusion.1
  92.5 0.8 copy.13
  93.4 0.0 reduce-scatter.9.cloned.1.call-update
  93.4 0.0 reduce-scatter.7.cloned.1.call-start
  93.4 0.0 copy-done.2
  93.4 0.0 copy-start.1
  93.5 34.1 %all_gather.6 = f32[256,256]{1,0:T(8,128)S(1)} all-gather(f32[16,256]{1,0:T(8,128)S(1)} %copy-done.2), channel_id=1, replica_groups=mesh['row'=16,'col'=32] {'row'}, dimensions={0}, use_global_device_ids=true | all-gather | bytes 278528 | tf_op jit(solution)/shard_map/all_gather | solution.py:56
  127.5 0.2 broadcast_multiply_fusion.1
  127.7 2.1 fusion.18
  129.8 2.1 convolution_add_fusion.6
  131.9 0.0 copy-done.1
  131.9 1.0 convolution_add_fusion.5
  133.0 1.0 convolution_add_fusion.4
  134.0 1.0 convolution_add_fusion.3
  135.1 1.0 convolution_add_fusion.2
  136.1 1.0 convolution_add_fusion.1
  137.2 1.0 fusion
  138.2 1.0 copy.11
  139.2 0.0 reduce-scatter.7.cloned.1.call-update
  139.2 27.8 %reduce-scatter.9.cloned.1.call-done = f32[16,256]{1,0:T(8,128)} async-done(((f32[256,256]{1,0:T(8,128)}), f32[16,256]{1,0:T(8,128)}) %reduce-scatter.9.cloned.1.call-update) | async-done | bytes 16400
  167.0 0.8 copy.14
  167.9 0.1 multiply_reduce_fusion
  168.0 635.2 %reduce-scatter.7.cloned.1.call-done = f32[16,256]{1,0:T(8,128)} async-done(((f32[512,256]{1,0:T(8,128)}), f32[16,256]{1,0:T(8,128)}) %reduce-scatter.7.cloned.1.call-update) | async-done | bytes 16400
  803.2 0.8 copy.12
  804.0 0.1 multiply_reduce_fusion.1
  804.1 112.8 %all-reduce = (f32[1,256]{1,0:T(1,128)S(1)}, f32[1,256]{1,0:T(1,128)S(1)}) all-reduce(f32[1,256]{1,0:T(1,128)S(1)} %bitcast.105, f32[1,256]{1,0:T(1,128)S(1)} %bitcast.106), channel_id=1, replica_groups=mesh['row'=16,'col'=32] {'row','col'}, use_global_device_ids=true, to_apply=%region_5.0 | all-reduce | flops 512 | bytes 4096 | tf_op jit(solution)/shard_map/psum | solution.py:68
  916.9 0.6 fusion.37
  (1 shorter events, 0.0 us)
Async XLA Ops:
  7.2 159.9 %reduce-scatter.9.cloned.1.call-start = ((), (), s32[]{:S(2)}) async-start(), calls=%async_computation.3 | async-start | bytes 278528
  82.0 2.2 copy-start
  87.3 6.1 copy-start.2
  93.4 709.8 %reduce-scatter.7.cloned.1.call-start = ((), (), s32[]{:S(2)}) async-start(), calls=%async_computation.2 | async-start | bytes 540672
  93.4 38.5 %copy-start.1 = (f32[8,512,256]{2,1,0:T(8,128)S(1)}, f32[8,512,256]{2,1,0:T(8,128)}, u32[]{:S(2)}) copy-start(f32[8,512,256]{2,1,0:T(8,128)} %param.4) | copy-start | bytes 12582916
Sparse Core Ops, SparseCore 0:
  93.5 73.4 reduce-scatter.8
  172.0 631.1 reduce-scatter.6
where the time goes:
time: 925 us; the launch traced here: 924 us
  waiting for transfers between devices  663 us (72%)
  blocking collectives  220 us (24%)
  matrix products  18.7 us (2%)
  between operations  14.2 us (2%)
    unnamed x4, waiting for transfers between devices  663 us
    psum x1, blocking collectives, body(): lax.psum((jnp.sum(right_resid * right_resid, axis=0), jnp.sum(left_resid...  113 us
    all_gather x1, blocking collectives, body(): left_rows = lax.all_gather(left_vecs, 'col', axis=0, tiled=True)  72.7 us
    all_gather x1, blocking collectives, body(): right_cols = lax.all_gather(right_vecs, 'row', axis=0, tiled=True)  34.1 us
  transfers between devices with their start and end apart: 2, of which 2 were waited for; matrix products, arithmetic and copies ran while one was open for 1% of the time, Pallas kernels for 0%

commit v1 on v0

--- a/solution.py
+++ b/solution.py
@@ -54,7 +54,9 @@
 def body(coefficients, lambdas, right_vecs, left_vecs):
     weights = chebyshev(lambdas, coefficients.shape[0])
     right_cols = lax.all_gather(right_vecs, "row", axis=0, tiled=True)
-    left_rows = lax.all_gather(left_vecs, "col", axis=0, tiled=True)
+    left_rows = jnp.concatenate(
+        lax.all_to_all(jnp.stack([left_vecs] * lax.axis_size("col")), "col", 0, 0), axis=0
+    )
     right_weighted = right_cols[None, :, :] * weights[:, None, :]
     left_weighted = left_rows[None, :, :] * weights[:, None, :]
     matrices = coefficients

time: 925 us -> 884 us (0.956)
  blocking collectives: 220 us -> 127 us
  waiting for transfers between devices: 663 us -> 694 us
  starting transfers between devices: 0.08 us -> 18.9 us
    all_gather x1 -> x0, blocking collectives: 72.7 us -> none  [body(): left_rows = lax.all_gather(left_vecs, 'col', axis=0, tiled=True)]
    unnamed x4, waiting for transfers between devices: 663 us -> 694 us
    all_to_all x0 -> x1, starting transfers between devices: none -> 18.6 us  [body(): lax.all_to_all(jnp.stack([left_vecs] * lax.axis_size('col')), 'col', 0, 0)]
    all_gather x1, blocking collectives: 34.1 us -> 20.6 us  [body(): right_cols = lax.all_gather(right_vecs, 'row', axis=0, tiled=True)]
  transfers between devices with their start and end apart: 2 -> 3, of which waited for: 2 -> 2; matrix products, arithmetic and copies ran while one was open for 1% -> 3% of each run, Pallas kernels for 0% -> 0%
where the time goes in v1:
time: 884 us; the launch traced here: 883 us
  waiting for transfers between devices  694 us (79%)
  blocking collectives  127 us (14%)
  starting transfers between devices  18.9 us (2%)
  matrix products  18.8 us (2%)
  between operations  14.2 us (2%)
    unnamed x4, waiting for transfers between devices  694 us
    psum x1, blocking collectives, body(): lax.psum((jnp.sum(right_resid * right_resid, axis=0), jnp.sum(left_resid...  106 us
    all_gather x1, blocking collectives, body(): right_cols = lax.all_gather(right_vecs, 'row', axis=0, tiled=True)  20.6 us
    all_to_all x1, starting transfers between devices, body(): lax.all_to_all(jnp.stack([left_vecs] * lax.axis_size('col')), 'col', 0, 0)  18.6 us
  transfers between devices with their start and end apart: 3, of which 2 were waited for; matrix products, arithmetic and copies ran while one was open for 3% of the time, Pallas kernels for 0%

profile of v1, /device:TPU:1, one launch (start us, length us, event | category | flops | bytes accessed | tf_op | source)
XLA Modules:
  0.0 883.3 jit_solution(4086444135071189958)
XLA Ops:
  7.2 1.6 stack.32
  8.8 18.6 %all-to-all-start = ((f32[32,16,256]{2,1,0:T(8,128)}), f32[32,16,256]{2,1,0:T(8,128)S(1)}, u32[]{:S(2)}, u32[]{:S(2)}) async-start(f32[32,16,256]{2,1,0:T(8,128)} %stack.32), calls=%async_computation | async-start | bytes 1048576 | tf_op jit(solution)/shard_map/all_to_all | solution.py:58
  27.4 0.0 reduce-scatter.7.cloned.1.call-start
  27.5 0.7 multiply_subtract_fusion
  28.2 0.7 multiply_subtract_fusion.1
  28.8 20.6 %all_gather.3 = f32[256,256]{1,0:T(8,128)S(1)} all-gather(f32[16,256]{1,0:T(8,128)} %param.6), channel_id=1, replica_groups=mesh['row'=16,'col'=32] {'row'}, dimensions={0}, use_global_device_ids=true | all-gather | bytes 278528 | tf_op jit(solution)/shard_map/all_gather | solution.py:56
  49.5 0.7 stack.31
  50.2 0.0 copy-start
  50.2 0.2 broadcast_multiply_fusion.1
  50.3 2.2 fusion.18
  52.6 2.1 convolution_add_fusion.6
  54.7 0.0 copy-done
  54.7 1.0 convolution_add_fusion.5
  55.7 1.0 convolution_add_fusion.4
  56.8 1.0 convolution_add_fusion.3
  57.9 1.0 convolution_add_fusion.2
  58.9 1.0 convolution_add_fusion.1
  60.0 1.0 fusion
  61.0 1.0 copy.11
  62.0 0.0 reduce-scatter.7.cloned.1.call-update
  62.0 0.2 reduce-scatter.9.cloned.1.call-start
  62.3 0.0 all-to-all-done
  62.3 0.0 copy-start.1
  62.3 0.4 broadcast_multiply_fusion
  62.6 1.8 copy-done.1
  64.5 1.0 fusion.2
  65.5 1.0 convolution_add_fusion.13
  66.5 1.0 convolution_add_fusion.12
  67.6 1.0 convolution_add_fusion.11
  68.6 1.0 convolution_add_fusion.10
  69.6 1.0 convolution_add_fusion.9
  70.7 1.0 convolution_add_fusion.8
  71.7 1.0 fusion.1
  72.7 0.8 copy.13
  73.6 0.0 reduce-scatter.9.cloned.1.call-update
  73.6 617.2 %reduce-scatter.7.cloned.1.call-done = f32[16,256]{1,0:T(8,128)} async-done(((f32[512,256]{1,0:T(8,128)}), f32[16,256]{1,0:T(8,128)}) %reduce-scatter.7.cloned.1.call-update) | async-done | bytes 16400
  690.8 0.8 copy.12
  691.6 0.1 multiply_reduce_fusion.1
  691.7 77.1 %reduce-scatter.9.cloned.1.call-done = f32[16,256]{1,0:T(8,128)} async-done(((f32[256,256]{1,0:T(8,128)}), f32[16,256]{1,0:T(8,128)}) %reduce-scatter.9.cloned.1.call-update) | async-done | bytes 16400
  768.8 0.8 copy.14
  769.7 0.1 multiply_reduce_fusion
  769.8 106.1 %all-reduce = (f32[1,256]{1,0:T(1,128)S(1)}, f32[1,256]{1,0:T(1,128)S(1)}) all-reduce(f32[1,256]{1,0:T(1,128)S(1)} %bitcast.108, f32[1,256]{1,0:T(1,128)S(1)} %bitcast.107), channel_id=1, replica_groups=mesh['row'=16,'col'=32] {'row','col'}, use_global_device_ids=true, to_apply=%region_5.0 | all-reduce | flops 512 | bytes 4096 | tf_op jit(solution)/shard_map/psum | solution.py:70
  875.9 0.6 fusion.37
  (1 shorter events, 0.0 us)
Async XLA Ops:
  8.8 53.5 %all-to-all-start = ((f32[32,16,256]{2,1,0:T(8,128)}), f32[32,16,256]{2,1,0:T(8,128)S(1)}, u32[]{:S(2)}, u32[]{:S(2)}) async-start(f32[32,16,256]{2,1,0:T(8,128)} %stack.32), calls=%async_computation | async-start | bytes 1048576 | tf_op jit(solution)/shard_map/all_to_all | solution.py:58
  27.4 663.4 %reduce-scatter.7.cloned.1.call-start = ((), (), s32[]{:S(2)}) async-start(), calls=%async_computation.3 | async-start | bytes 540672
  50.2 4.5 copy-start
  62.0 706.8 %reduce-scatter.9.cloned.1.call-start = ((), (), s32[]{:S(2)}) async-start(), calls=%async_computation.4 | async-start | bytes 278528
  62.3 2.2 copy-start.1
Sparse Core Ops, SparseCore 0:
  62.1 628.5 reduce-scatter.6
  694.1 74.6 reduce-scatter.8
